TPU v7x, 32 devices: a whole 2x2x4 slice. The times are simulated.
32 devices in a mesh: prow: 4 (over y, core), pcol: 8 (over z, x).
Axes of the slice: x: 2, y: 2, z: 4, core: 2. Of those that a mesh axis runs over, the one named last changes fastest.
Arguments:
- matrix: bfloat16 [4096, 2048], P('prow', 'pcol'), may hold values from -6 to 6
- panel_one: bfloat16 [256, 4096], P('pcol', 'prow'), may hold values from -0.375 to 0.375
- panel_two: bfloat16 [256, 4096], P('pcol', 'prow'), may hold values from -0.375 to 0.375
- pivots_one: int32 [256], replicated, may hold values from 0 to 4095, as said below
- pivots_two: int32 [256], replicated, may hold values from 256 to 4095, as said below
Outputs:
- trailing: bfloat16 [4096, 2048], P('prow', 'pcol')
Inputs may be any that keep to these rules, and one draw needn't show every extreme that they name: Each pivots_one[i] is either i or a logical row from 256 to 4095; no row is named twice; 4095 is always named. Each pivots_two[i] is either 256 + i or a logical row from 512 to 4095; no row is named twice; 4095 is always named.
All inputs are finite; a program needn't handle non-finite values.
Results may differ from a plain program's by a relative error of at most 0.006.
Values may be sent and summed in bfloat16 or wider, within the bound.
A program may use at most 64 MiB of HBM per device.

v0:
```python
import jax
import jax.numpy as jnp
from jax import lax
from jax.sharding import PartitionSpec as P


def spread(block, axis, source):
    block = jnp.where(lax.axis_index(axis) == source, block, jnp.zeros_like(block))
    return lax.psum(block, axis)


def logical_rows(local_rows, row_index, process_rows, width):
    return (local_rows // width * process_rows + row_index) * width + local_rows % width


def stored_place(logical, process_rows, width):
    owner_row = logical // width % process_rows
    local_row = logical // width // process_rows * width + logical % width
    return (owner_row, local_row)


def trade_order(pivots, first_row, total_rows):
    width = pivots.shape[0]
    order_map = jnp.arange(total_rows, dtype=jnp.int32)
    pivot_at = first_row + jnp.arange(width, dtype=jnp.int32)
    order_map = order_map.at[pivots].set(pivot_at)
    return order_map.at[pivot_at].set(pivots)


def swap_local(current, old_block, order_map, logical, first_row, width):
    source = jnp.take(order_map, logical)
    is_moved = (logical >= first_row + width) & (source != logical)
    filled = jnp.take(old_block, jnp.clip(source - first_row, 0, width - 1), axis=0)
    return jnp.where(is_moved[:, None], filled, current)


def unit_inverse(strict):
    extent = strict.shape[0]
    identity = jnp.eye(extent, dtype=jnp.float32)
    result = identity - strict
    powered = strict
    for repeat in range((extent - 1).bit_length() - 1):
        powered = jnp.dot(powered, powered, precision=lax.Precision.HIGHEST)
        result = jnp.dot(result, identity + powered, precision=lax.Precision.HIGHEST)
    return result


def pivot_solve(incoming, diagonal, section_index, process_rows):
    strict = jnp.tril(diagonal.T.astype(jnp.float32), -1)
    solved = jnp.dot(
        unit_inverse(strict), incoming.astype(jnp.float32), precision=lax.Precision.HIGHEST
    ).astype(jnp.bfloat16)
    solved = spread(solved, "prow", section_index % process_rows)
    return solved


def collect(picker, order_map, first_row, section_index, row_index, process_rows, width):
    sources = order_map[first_row : first_row + width]
    owner_row, local_row = stored_place(sources, process_rows, width)
    is_mine = (owner_row == row_index).astype(jnp.float32)[:, None]
    arriving = picker(local_row).astype(jnp.float32) * is_mine
    block_local = section_index // process_rows * width + jnp.arange(width, dtype=jnp.int32)
    holder = (row_index == section_index % process_rows).astype(jnp.float32)
    leaving = picker(block_local).astype(jnp.float32) * holder
    summed = lax.psum(
        jnp.concatenate([arriving, leaving], axis=0).astype(jnp.bfloat16), "prow"
    ).astype(jnp.float32)
    incoming = summed[:width].astype(jnp.bfloat16)
    old_block = summed[width:].astype(jnp.bfloat16)
    return (incoming, old_block)


def finish(swapped, solved, panel_all, logical, first_row, width):
    product = lax.dot_general(
        panel_all, solved, (((0,), (0,)), ((), ())), preferred_element_type=jnp.float32
    )
    updated = (swapped.astype(jnp.float32) - product).astype(jnp.bfloat16)
    pivot_part = jnp.take(solved, jnp.clip(logical - first_row, 0, width - 1), axis=0)
    in_block = (logical >= first_row) & (logical < first_row + width)
    beyond = logical >= first_row + width
    return jnp.where(beyond[:, None], updated, jnp.where(in_block[:, None], pivot_part, swapped))


def on_device(matrix, panel_one, panel_two, pivots_one, pivots_two):
    rows_dev = matrix.shape[0]
    process_rows = lax.axis_size("prow")
    row_index = lax.axis_index("prow")
    width = panel_one.shape[0] * lax.axis_size("pcol")
    total_rows = rows_dev * process_rows
    logical = logical_rows(jnp.arange(rows_dev, dtype=jnp.int32), row_index, process_rows, width)
    start_two = 1 // process_rows * width
    panel_all_one, panel_all_two = (
        lax.all_gather(panel_one, "pcol", axis=0, tiled=True),
        lax.all_gather(panel_two, "pcol", axis=0, tiled=True),
    )
    diagonal_one = panel_all_one[:, 0:width]
    diagonal_two = panel_all_two[:, start_two : start_two + width]
    order_one = trade_order(pivots_one, 0, total_rows)
    order_two = trade_order(pivots_two, width, total_rows)
    incoming_one, old_one = collect(
        lambda local_row: jnp.take(matrix, local_row, axis=0),
        order_one,
        0,
        0,
        row_index,
        process_rows,
        width,
    )
    swapped_one = swap_local(matrix, old_one, order_one, logical, 0, width)
    solved_one = pivot_solve(incoming_one, diagonal_one, 0, process_rows)
    after_one = finish(swapped_one, solved_one, panel_all_one, logical, 0, width)
    incoming_two, old_two = collect(
        lambda local_row: jnp.take(after_one, local_row, axis=0),
        order_two,
        width,
        1,
        row_index,
        process_rows,
        width,
    )
    swapped_two = swap_local(after_one, old_two, order_two, logical, width, width)
    solved_two = pivot_solve(incoming_two, diagonal_two, 1, process_rows)
    return finish(swapped_two, solved_two, panel_all_two, logical, width, width)


def solution(mesh):
    placed = (P("prow", "pcol"), P("pcol", "prow"), P("pcol", "prow"), P(), P())
    return jax.shard_map(
        on_device, mesh=mesh, in_specs=placed, out_specs=P("prow", "pcol"), check_vma=False
    )
```

profile of v0, /device:TPU:12, one launch (start us, length us, event | category | flops | bytes accessed | tf_op | source)
XLA Modules:
  0.0 228.3 jit_solution(7140232656776959476)
XLA Ops:
  7.2 1.4 scatter_fusion.2
  8.7 1.4 scatter_fusion.3
  10.3 1.2 gather_fusion.2
  11.4 1.2 gather_fusion.3
  14.3 28.7 %all_gather.6 = bf16[256,1024]{1,0:T(8,128)(2,1)S(1)} all-gather(bf16[32,1024]{1,0:T(8,128)(2,1)S(1)} %copy-done.3), channel_id=1, replica_groups=mesh['prow'=4,'pcol'=8] {'pcol'}, dimensions={0}, use_global_device_ids=true | all-gather | bytes 589824 | tf_op jit(solution)/shard_map/all_gather | solution.py:93
  44.5 6.2 %gather_fusion.1 = s32[1024]{0:T(1024)S(1)} fusion(s32[4096]{0:T(1024)S(1)} %scatter_fusion.3, s32[1024]{0:T(1024)S(1)} %fusion.43), kind=kCustom, calls=%fused_computation.3.clone | custom fusion | bytes 12288 | tf_op jit(solution)/shard_map/jit(_take)/gather | solution.py:31
  51.4 1.4 scatter_fusion
  52.8 1.4 scatter_fusion.1
  54.3 6.2 %gather_fusion = s32[1024]{0:T(1024)S(1)} fusion(s32[4096]{0:T(1024)S(1)} %scatter_fusion.1, s32[1024]{0:T(1024)S(1)} %fusion.43), kind=kCustom, calls=%fused_computation.clone | custom fusion | bytes 12288 | tf_op jit(solution)/shard_map/jit(_take)/gather | solution.py:31
  60.5 31.5 %all_gather.7 = bf16[256,1024]{1,0:T(8,128)(2,1)S(1)} all-gather(bf16[32,1024]{1,0:T(8,128)(2,1)S(1)} %copy-done.4), channel_id=1, replica_groups=mesh['prow'=4,'pcol'=8] {'pcol'}, dimensions={0}, use_global_device_ids=true | all-gather | bytes 589824 | tf_op jit(solution)/shard_map/all_gather | solution.py:94
  102.4 1.8 fusion.6
  105.5 3.9 %gather_fusion.4 = bf16[1024,256]{1,0:T(8,128)(2,1)S(1)} fusion(bf16[256,256]{1,0:T(8,128)(2,1)S(1)} %slice-done, s32[1024]{0:T(1024)S(1)} %get-tuple-element.23), kind=kCustom, calls=%fused_computation.2.clone | custom fusion | bytes 1052672 | tf_op jit(solution)/shard_map/jit(_take)/gather | solution.py:33
  109.4 1.0 copy.26
  110.5 28.4 %all-reduce.7.cloned.1.call-done = bf16[256,256]{1,0:T(8,128)(2,1)} async-done(((bf16[256,256]{1,0:T(8,128)(2,1)}), bf16[256,256]{1,0:T(8,128)(2,1)}) %all-reduce.7.cloned.1.call-update) | async-done | bytes 131088 | tf_op jit(solution)/shard_map/psum | solution.py:9
  138.8 4.4 %gather_fusion.5 = bf16[1024,256]{1,0:T(8,128)(2,1)S(1)} fusion(bf16[256,256]{1,0:T(8,128)(2,1)} %all-reduce.7.cloned.1.call-done, s32[1024]{0:T(1024)S(1)} %get-tuple-element.22), kind=kCustom, calls=%fused_computation.7.clone | custom fusion | bytes 1052672 | tf_op jit(solution)/shard_map/jit(_take)/gather | solution.py:78
  143.2 1.0 copy.29
  144.2 1.5 fusion.5
  146.0 1.2 gather_fusion.7
  147.1 1.2 gather_fusion.6
  149.4 32.0 %all-reduce.9.cloned.1.call-done = bf16[512,256]{1,0:T(8,128)(2,1)} async-done(((bf16[512,256]{1,0:T(8,128)(2,1)}), bf16[512,256]{1,0:T(8,128)(2,1)}) %all-reduce.9.cloned.1.call-update) | async-done | bytes 262160 | tf_op jit(solution)/shard_map/psum | solution.py:65
  181.3 1.8 fusion.7
  184.1 3.9 %gather_fusion.8 = bf16[1024,256]{1,0:T(8,128)(2,1)S(1)} fusion(bf16[256,256]{1,0:T(8,128)(2,1)S(1)} %slice-done.1, s32[1024]{0:T(1024)S(1)} %get-tuple-element.25), kind=kCustom, calls=%fused_computation.8.clone | custom fusion | bytes 1052672 | tf_op jit(solution)/shard_map/jit(_take)/gather | solution.py:33
  188.3 26.8 %all-reduce.11.cloned.1.call-done = bf16[256,256]{1,0:T(8,128)(2,1)} async-done(((bf16[256,256]{1,0:T(8,128)(2,1)}), bf16[256,256]{1,0:T(8,128)(2,1)}) %all-reduce.11.cloned.1.call-update) | async-done | bytes 131088 | tf_op jit(solution)/shard_map/psum | solution.py:9
  215.1 4.4 %gather_fusion.9 = bf16[1024,256]{1,0:T(8,128)(2,1)S(1)} fusion(bf16[256,256]{1,0:T(8,128)(2,1)} %all-reduce.11.cloned.1.call-done, s32[1024]{0:T(1024)S(1)} %get-tuple-element.24), kind=kCustom, calls=%fused_computation.9.clone | custom fusion | bytes 1052672 | tf_op jit(solution)/shard_map/jit(_take)/gather | solution.py:78
  (97 shorter events, 20.7 us)
Async XLA Ops:
  6.5 95.9 %all-reduce.5.cloned.1.call-start = ((), (), s32[]{:S(2)}) async-start(), calls=%async_computation | async-start | bytes 524288 | tf_op jit(solution)/shard_map/psum | solution.py:65
  6.5 0.7 copy-start.5
  8.7 1.6 copy-start.2
  13.5 0.8 copy-start.3
  13.5 125.3 %all-reduce.7.cloned.1.call-start = ((), (), s32[]{:S(2)}) async-start(), calls=%async_computation.1 | async-start | bytes 262144 | tf_op jit(solution)/shard_map/psum | solution.py:9
  50.7 0.7 copy-start.6
  54.3 6.2 %copy-start.4 = (bf16[32,1024]{1,0:T(8,128)(2,1)S(1)}, bf16[32,1024]{1,0:T(8,128)(2,1)}, u32[]{:S(2)}) copy-start(bf16[32,1024]{1,0:T(8,128)(2,1)} %param.13) | copy-start | bytes 196612
  104.3 77.0 %all-reduce.9.cloned.1.call-start = ((), (), s32[]{:S(2)}) async-start(), calls=%async_computation.2 | async-start | bytes 524288 | tf_op jit(solution)/shard_map/psum | solution.py:65
  104.6 0.9 slice-start
  143.2 1.0 copy-start
  149.3 65.8 %all-reduce.11.cloned.1.call-start = ((), (), s32[]{:S(2)}) async-start(), calls=%async_computation.3 | async-start | bytes 262144 | tf_op jit(solution)/shard_map/psum | solution.py:9
  183.2 0.9 slice-start.1
  219.5 0.9 copy-start.1
Sparse Core Ops, SparseCore 0:
  13.6 32.0 all-reduce.4
  104.4 34.3 all-reduce.6
  149.4 31.8 all-reduce.8
  183.6 31.4 all-reduce.10
where the time goes:
time: 231 us; the launch traced here: 228 us
  waiting for transfers between devices  87.2 us (38%)
  blocking collectives  60.2 us (26%)
  local copies, waits for them, and re-layouts  48 us (21%)
  matrix products  16.7 us (7%)
  between operations  13.7 us (6%)
    psum x2, waiting for transfers between devices, spread(): return lax.psum(block, axis)  55.2 us
    psum x2, waiting for transfers between devices, collect(): lax.psum(jnp.concatenate([arriving, leaving], axis=0).astype(jnp.bfloat16...  32 us
    all_gather x1, blocking collectives, on_device(): lax.all_gather(panel_two, 'pcol', axis=0, tiled=True)  31.5 us
    all_gather x1, blocking collectives, on_device(): lax.all_gather(panel_one, 'pcol', axis=0, tiled=True)  28.7 us
    gather x2, local copies, waits for them, and re-layouts, swap_local(): source = jnp.take(order_map, logical)  12.3 us
    gather x4, local copies, waits for them, and re-layouts, finish(): jnp.take(solved, jnp.clip(logical - first_row, 0, width - 1), axis=0)  9.97 us
    gather x4, local copies, waits for them, and re-layouts, swap_local(): jnp.take(old_block, jnp.clip(source - first_row, 0, width - 1), axis=0)  9.09 us
    dot_general x14, matrix products, unit_inverse(): jnp.dot(result, identity + powered, precision=lax.Precision.HIGHEST)  5.61 us
  transfers between devices with their start and end apart: 4, of which 3 were waited for; matrix products, arithmetic and copies ran while one was open for 16% of the time, Pallas kernels for 0%

commit v1 on v0

v1 whole, which is shorter than its diff:
```python
import functools

import jax
import jax.numpy as jnp
from jax import lax
from jax.experimental import pallas as pl
from jax.experimental.pallas import tpu as pltpu
from jax.sharding import PartitionSpec as P

F32 = jnp.float32
BF16 = jnp.bfloat16
ROW_ROW = (((0,), (0,)), ((), ()))


def dot(a, b):
    return jnp.dot(a, b, preferred_element_type=F32)


def dot_t(a, b):
    return lax.dot_general(a, b, ROW_ROW, preferred_element_type=F32)


def halves(a):
    high = a.astype(BF16)
    return high, (a - high.astype(F32)).astype(BF16)


def dot_split(a, b):
    a_high, a_low = halves(a)
    b_high, b_low = halves(b)
    return dot(a_high, b_high) + (dot(a_high, b_low) + dot(a_low, b_high))


def unit_inverse(diagonal):
    extent = diagonal.shape[0]
    row = lax.broadcasted_iota(jnp.int32, (extent, extent), 0)
    col = lax.broadcasted_iota(jnp.int32, (extent, extent), 1)
    strict = jnp.where(row > col, diagonal.astype(F32).T, 0.0)
    exact = strict.astype(BF16)
    powered = dot(exact, exact)
    result = jnp.where(row == col, 1.0, 0.0) - strict
    repeats = (extent - 1).bit_length() - 1
    for repeat in range(repeats):
        if repeat == repeats - 1:
            return result + dot_split(result, powered)
        both = dot_split(jnp.concatenate([result, powered], axis=0), powered)
        result, powered = result + both[:extent], both[extent:]
    return result


def solve(inverse, incoming):
    high, low = halves(inverse)
    return (dot(high, incoming) + dot(low, incoming)).astype(BF16)


def onehot(a, b):
    return (a == b).astype(F32)


def body(
    process_rows, process_cols,
    matrix, panel_one, panel_two, piv_one, piv_two, out,
    gathered, sent_rows, rows_in, block_in, sent_sel, sel_in, aux,
    g_send, g_recv, f_send, r_send, r_recv, b_send, b_recv, s_send, s_recv, d_send, d_recv,
):
    width = piv_one.shape[1]
    rows_dev = matrix.shape[0]
    shard = panel_one.shape[0]
    size_z = process_cols // 2
    my_row = lax.axis_index("prow")
    my_col = lax.axis_index("pcol")
    my_z, my_x = my_col // 2, my_col % 2
    x_peer = my_z * 2 + (1 - my_x)

    def row_peer(step):
        return lax.rem(my_row + step, process_rows)

    def z_peer(step):
        return lax.rem(my_z + step, size_z) * 2 + my_x

    barrier = pltpu.get_barrier_semaphore()
    for step in range(1, process_rows):
        pl.semaphore_signal(barrier, 1, device_id={"prow": row_peer(step)}, device_id_type=pl.DeviceIdType.MESH)
    for step in range(1, size_z):
        pl.semaphore_signal(barrier, 1, device_id={"pcol": z_peer(step)}, device_id_type=pl.DeviceIdType.MESH)
    pl.semaphore_signal(barrier, 1, device_id={"pcol": x_peer}, device_id_type=pl.DeviceIdType.MESH)

    local = lax.broadcasted_iota(jnp.int32, (rows_dev, width), 0)
    logical = (local // width * process_rows + my_row) * width + local % width
    hit_one = onehot(logical, piv_one[...])
    hit_two = onehot(logical, piv_two[...])
    pick_one, pick_two = hit_one.astype(BF16), hit_two.astype(BF16)
    sent_sel[...] = dot(panel_one[...], pick_two).astype(BF16)
    gathered[0, my_col] = panel_one[...]
    gathered[2, my_col] = panel_two[...]

    pl.semaphore_wait(barrier, process_rows - 1 + size_z)

    def remote(src, dst, send, recv, device):
        return pltpu.make_async_remote_copy(
            src_ref=src, dst_ref=dst, send_sem=send, recv_sem=recv,
            device_id=device, device_id_type=pl.DeviceIdType.MESH,
        )

    def sel_copy(step):
        return remote(sent_sel, sel_in.at[my_row], s_send.at[step], s_recv.at[my_row], {"prow": row_peer(step)})

    def fixed_copy(which, step):
        src = (panel_one, panel_one, panel_two)[which].at[:, pl.ds(0, width)]
        dst = aux.at[which]
        return remote(src, dst, d_send.at[which, step], d_recv.at[which], {"prow": row_peer(step)})

    def block_copy(which, step):
        src = matrix.at[pl.ds(0, width), :]
        return remote(src, block_in.at[which], b_send.at[which, step], b_recv.at[which], {"prow": row_peer(step)})

    def rows_copy(which, step):
        return remote(
            sent_rows.at[which], rows_in.at[which, my_row],
            r_send.at[which, step], r_recv.at[which, my_row], {"prow": row_peer(step)},
        )

    def gather_copy(array, step):
        dst = gathered.at[array, my_col]
        device = {"pcol": z_peer(step) if step else x_peer}
        return remote(dst, dst, g_send.at[array, step], g_recv.at[array, my_col], device)

    def forward_copy(array, step):
        slot = gathered.at[array, z_peer(step)]
        return remote(slot, slot, f_send.at[array, step], g_recv.at[array, z_peer(step)], {"pcol": x_peer})

    def arrive(array, col):
        slot = gathered.at[array, col]
        remote(slot, slot, g_send.at[array, 0], g_recv.at[array, col], {"pcol": x_peer}).wait_recv()

    peers = range(1, process_rows)
    holders = (0, 1, 1)
    for step in peers:
        sel_copy(step).start()
    for which in range(3):
        @pl.when(my_row == holders[which])
        def _(which=which):
            for step in peers:
                fixed_copy(which, step).start()
            aux[which] = (panel_one, panel_one, panel_two)[which][:, pl.ds(0, width)]

    for step in range(size_z):
        gather_copy(0, step).start()

    sent_rows[0] = dot_t(pick_one, matrix[...]).astype(BF16)
    for step in peers:
        rows_copy(0, step).start()
    sent_rows[1] = dot_t(pick_two, matrix[...]).astype(BF16)
    for step in peers:
        rows_copy(1, step).start()
    for which in range(2):
        @pl.when(my_row == which)
        def _(which=which):
            for step in peers:
                block_copy(which, step).start()
            block_in[which] = matrix[pl.ds(0, width), :]

    selected = sent_sel[...].astype(F32)
    for step in peers:
        source = row_peer(step)
        slot = sel_in.at[source]
        remote(slot, slot, s_send.at[0], s_recv.at[source], {"prow": source}).wait_recv()
        selected = selected + sel_in[source].astype(F32)
    for which in range(3):
        @pl.when(my_row != holders[which])
        def _(which=which):
            slot = aux.at[which]
            remote(slot, slot, d_send.at[which, 0], d_recv.at[which], {"prow": row_peer(1)}).wait_recv()
    for which in range(3):
        gathered[1, my_col, :, pl.ds(which * width, width)] = aux[which]
    gathered[1, my_col, :, pl.ds(3 * width, width)] = selected.astype(BF16)
    for array in (1, 2):
        for step in range(size_z):
            gather_copy(array, step).start()

    def take_z(array):
        for step in range(1, size_z):
            arrive(array, z_peer(step))
            forward_copy(array, step).start()

    def take_x(array):
        for step in range(size_z):
            arrive(array, lax.rem(my_z + step, size_z) * 2 + (1 - my_x))

    def whole(array, start, count):
        return gathered[array, :, :, pl.ds(start, count)].reshape(process_cols * shard, count)

    take_z(0)
    take_z(1)
    take_x(1)
    inverse_one = unit_inverse(whole(1, 0, width))
    inverse_two = unit_inverse(whole(1, 2 * width, width))
    take_z(2)

    def summed(which):
        total = sent_rows[which].astype(F32)
        for step in peers:
            source = row_peer(step)
            slot = rows_in.at[which, source]
            remote(slot, slot, r_send.at[which, 0], r_recv.at[which, source], {"prow": source}).wait_recv()
            total = total + rows_in[which, source].astype(F32)
        return total

    for which in range(2):
        @pl.when(my_row != which)
        def _(which=which):
            slot = block_in.at[which]
            remote(slot, slot, b_send.at[which, 0], b_recv.at[which], {"prow": row_peer(1)}).wait_recv()

    solved_one = solve(inverse_one, summed(0).astype(BF16))
    leaving_one = block_in[0]

    first_row = width
    first_across = jnp.broadcast_to(piv_one[...], (width, width))
    second_down = jnp.broadcast_to(piv_two[...].astype(F32), (width, width)).T.astype(jnp.int32)
    block_down = first_row + lax.broadcasted_iota(jnp.int32, (width, width), 0)

    def after_one(base, names, columns):
        match = onehot(names, first_across)
        moved = jnp.sum(match, axis=1, keepdims=True)
        swapped = base * (1.0 - moved) + dot(match.astype(BF16), leaving_one)
        return (swapped - dot_t(columns, solved_one)).astype(BF16)

    incoming_two = after_one(summed(1), second_down, whole(1, 3 * width, width))
    leaving_two = after_one(block_in[1].astype(F32), block_down, whole(1, width, width))
    solved_two = solve(inverse_two, incoming_two)

    take_x(0)
    moved_one = jnp.sum(hit_one, axis=1, keepdims=True)
    moved_two = jnp.sum(hit_two, axis=1, keepdims=True)
    swapped = matrix[...].astype(F32) * (1.0 - moved_one) + dot(pick_one, leaving_one)
    current = (swapped - dot_t(whole(0, 0, rows_dev), solved_one)).astype(BF16).astype(F32)
    swapped = current * (1.0 - moved_two) + dot(pick_two, leaving_two)
    take_x(2)
    out[...] = (swapped - dot_t(whole(2, 0, rows_dev), solved_two)).astype(BF16)

    @pl.when(my_row == 0)
    def _():
        out[pl.ds(0, width), :] = solved_one

    @pl.when(my_row == 1)
    def _():
        out[pl.ds(0, width), :] = solved_two

    for step in peers:
        sel_copy(step).wait_send()
        rows_copy(0, step).wait_send()
        rows_copy(1, step).wait_send()
    for which in range(3):
        @pl.when(my_row == holders[which])
        def _(which=which):
            for step in peers:
                fixed_copy(which, step).wait_send()
    for which in range(2):
        @pl.when(my_row == which)
        def _(which=which):
            for step in peers:
                block_copy(which, step).wait_send()
    for array in range(3):
        for step in range(size_z):
            gather_copy(array, step).wait_send()
        for step in range(1, size_z):
            forward_copy(array, step).wait_send()


def on_device(matrix, panel_one, panel_two, pivots_one, pivots_two):
    process_rows = lax.axis_size("prow")
    process_cols = lax.axis_size("pcol")
    shard, rows_dev = panel_one.shape
    width = pivots_one.shape[0]
    cols = matrix.shape[1]
    vmem = pl.BlockSpec(memory_space=pltpu.VMEM)
    dma = pltpu.SemaphoreType.DMA
    assert 4 * width == rows_dev and shard * process_cols == width and process_cols % 2 == 0
    size_z = process_cols // 2
    return pl.pallas_call(
        functools.partial(body, process_rows, process_cols),
        out_shape=jax.ShapeDtypeStruct(matrix.shape, BF16),
        in_specs=[vmem] * 5,
        out_specs=vmem,
        scratch_shapes=[
            pltpu.VMEM((3, process_cols, shard, rows_dev), BF16),
            pltpu.VMEM((2, width, cols), BF16),
            pltpu.VMEM((2, process_rows, width, cols), BF16),
            pltpu.VMEM((2, width, cols), BF16),
            pltpu.VMEM((shard, width), BF16),
            pltpu.VMEM((process_rows, shard, width), BF16),
            pltpu.VMEM((3, shard, width), BF16),
            dma((3, size_z)), dma((3, process_cols)), dma((3, size_z)),
            dma((2, process_rows)), dma((2, process_rows)),
            dma((2, process_rows)), dma((2,)),
            dma((process_rows,)), dma((process_rows,)),
            dma((3, process_rows)), dma((3,)),
        ],
        compiler_params=pltpu.CompilerParams(
            collective_id=0, has_side_effects=True, vmem_limit_bytes=40 * 1024 * 1024
        ),
    )(matrix, panel_one, panel_two, pivots_one.reshape(1, width), pivots_two.reshape(1, width))


def solution(mesh):
    placed = (P("prow", "pcol"), P("pcol", "prow"), P("pcol", "prow"), P(), P())
    return jax.shard_map(
        on_device, mesh=mesh, in_specs=placed, out_specs=P("prow", "pcol"), check_vma=False
    )
```

time: 231 us -> 41.3 us (0.18)
  waiting for transfers between devices: 87.2 us -> 0 us
  blocking collectives: 60.2 us -> 0 us
  local copies, waits for them, and re-layouts: 48 us -> 4.21 us
  Pallas kernels: 0 us -> 36.3 us
  matrix products: 16.7 us -> 0 us
  between operations: 13.7 us -> 0.01 us
    psum x4 -> x0, waiting for transfers between devices: 87.2 us -> none  [the longest x2 55.2 us: spread(): return lax.psum(block, axis)]
    all_gather x2 -> x0, blocking collectives: 60.2 us -> none  [the longest x1 31.5 us: on_device(): lax.all_gather(panel_two, 'pcol', axis=0, tiled=True)]
    pallas_call x0 -> x1, Pallas kernels: none -> 36.3 us  [on_device(): pl.pallas_call(functools.partial(body, process_rows, process_cols), out_s...]
    gather x14 -> x0, local copies, waits for them, and re-layouts: 36 us -> none  [the longest x2 12.3 us: swap_local(): source = jnp.take(order_map, logical)]
    dot_general x32 -> x0, matrix products: 16.7 us -> none  [the longest x14 5.61 us: unit_inverse(): jnp.dot(result, identity + powered, precision=lax.Precision.HIGHEST)]
    scatter x4 -> x0, local copies, waits for them, and re-layouts: 5.75 us -> none  [the longest x2 2.88 us: trade_order(): return order_map.at[pivot_at].set(pivots)]
  transfers between devices with their start and end apart: 4 -> 0, of which waited for: 3 -> 0; matrix products, arithmetic and copies ran while one was open for 16% -> 0% of each run, Pallas kernels for 0% -> 0%
where the time goes in v1:
time: 41.3 us; the launch traced here: 40.5 us
  Pallas kernels  36.3 us (88%)
  local copies, waits for them, and re-layouts  4.21 us (10%)
    pallas_call x1, Pallas kernels, on_device(): pl.pallas_call(functools.partial(body, process_rows, process_cols), out_s...  36.3 us
    unnamed x11, local copies, waits for them, and re-layouts  4.21 us

profile of v1, /device:TPU:12, one launch (start us, length us, event | category | flops | bytes accessed | tf_op | source)
XLA Modules:
  0.0 40.5 jit_solution(2540447355506854589)
XLA Ops:
  0.0 0.0 copy-start.4
  0.0 0.0 copy-start.3
  0.0 0.7 %copy-done.4 = s32[256]{0:T(256)S(1)} copy-done((s32[256]{0:T(256)S(1)}, s32[256]{0:T(256)}, u32[]{:S(2)}) %copy-start.4) | copy-done | bytes 1048
  0.7 0.0 copy-done.3
  0.7 0.0 copy-start
  0.7 1.0 %copy-done = bf16[1024,256]{1,0:T(8,128)(2,1)S(1)} copy-done((bf16[1024,256]{1,0:T(8,128)(2,1)S(1)}, bf16[1024,256]{1,0:T(8,128)(2,1)}, u32[]{:S(2)}) %copy-start) | copy-done | bytes 524312
  1.7 0.0 copy-start.1
  1.7 0.8 %copy-done.1 = bf16[32,1024]{1,0:T(8,128)(2,1)S(1)} copy-done((bf16[32,1024]{1,0:T(8,128)(2,1)S(1)}, bf16[32,1024]{1,0:T(8,128)(2,1)}, u32[]{:S(2)}) %copy-start.1) | copy-done | bytes 65560
  2.6 0.0 copy-start.2
  2.6 0.8 %copy-done.2 = bf16[32,1024]{1,0:T(8,128)(2,1)S(1)} copy-done((bf16[32,1024]{1,0:T(8,128)(2,1)S(1)}, bf16[32,1024]{1,0:T(8,128)(2,1)}, u32[]{:S(2)}) %copy-start.2) | copy-done | bytes 65560
  3.4 36.3 %shard_map.55 = bf16[1024,256]{1,0:T(8,128)(2,1)S(1)} custom-call(bf16[1024,256]{1,0:T(8,128)(2,1)S(1)} %copy-done, bf16[32,1024]{1,0:T(8,128)(2,1)S(1)} %copy-done.1, bf16[32,1024]{1,0:T(8,128)(2,1)S(1)} %copy-done.2, s32[1,256]{1,0:T(1,128)S(1)} %bitcast.2, s32[1,256]{1,0:T(1,128)S(1)} %bitcast.3), custom_call_target="tpu_custom_call" | custom-call | tf_op jit(solution)/shard_map/pallas_call | solution.py:281
  39.8 0.8 %copy.7 = bf16[1024,256]{1,0:T(8,128)(2,1)} copy(bf16[1024,256]{1,0:T(8,128)(2,1)S(1)} %shard_map.55) | data formatting | bytes 1048576
Async XLA Ops:
  0.0 0.7 %copy-start.4 = (s32[256]{0:T(256)S(1)}, s32[256]{0:T(256)}, u32[]{:S(2)}) copy-start(s32[256]{0:T(256)} %param.9) | copy-start | bytes 3076
  0.0 0.7 %copy-start.3 = (s32[256]{0:T(256)S(1)}, s32[256]{0:T(256)}, u32[]{:S(2)}) copy-start(s32[256]{0:T(256)} %param.8) | copy-start | bytes 3076
  0.7 1.0 %copy-start = (bf16[1024,256]{1,0:T(8,128)(2,1)S(1)}, bf16[1024,256]{1,0:T(8,128)(2,1)}, u32[]{:S(2)}) copy-start(bf16[1024,256]{1,0:T(8,128)(2,1)} %matrix.1) | copy-start | bytes 1572868
  1.7 0.8 %copy-start.1 = (bf16[32,1024]{1,0:T(8,128)(2,1)S(1)}, bf16[32,1024]{1,0:T(8,128)(2,1)}, u32[]{:S(2)}) copy-start(bf16[32,1024]{1,0:T(8,128)(2,1)} %panel_one.1) | copy-start | bytes 196612
  2.6 0.8 %copy-start.2 = (bf16[32,1024]{1,0:T(8,128)(2,1)S(1)}, bf16[32,1024]{1,0:T(8,128)(2,1)}, u32[]{:S(2)}) copy-start(bf16[32,1024]{1,0:T(8,128)(2,1)} %panel_two.1) | copy-start | bytes 196612

commit v2 on v1

v2 whole, which is shorter than its diff:
```python
import functools

import jax
import jax.numpy as jnp
from jax import lax
from jax.experimental import pallas as pl
from jax.experimental.pallas import tpu as pltpu
from jax.sharding import PartitionSpec as P

F32 = jnp.float32
BF16 = jnp.bfloat16
ROW_ROW = (((0,), (0,)), ((), ()))


def dot(a, b):
    return jnp.dot(a, b, preferred_element_type=F32)


def dot_t(a, b):
    return lax.dot_general(a, b, ROW_ROW, preferred_element_type=F32)


def halves(a):
    high = a.astype(BF16)
    return high, (a - high.astype(F32)).astype(BF16)


def dot_split(a, b):
    a_high, a_low = halves(a)
    b_high, b_low = halves(b)
    return dot(a_high, b_high) + (dot(a_high, b_low) + dot(a_low, b_high))


def unit_inverse(diagonal):
    extent = diagonal.shape[0]
    row = lax.broadcasted_iota(jnp.int32, (extent, extent), 0)
    col = lax.broadcasted_iota(jnp.int32, (extent, extent), 1)
    strict = jnp.where(row > col, diagonal.astype(F32).T, 0.0)
    exact = strict.astype(BF16)
    powered = dot(exact, exact)
    result = jnp.where(row == col, 1.0, 0.0) - strict
    repeats = (extent - 1).bit_length() - 1
    for repeat in range(repeats):
        if repeat == repeats - 1:
            return result + dot_split(result, powered)
        both = dot_split(jnp.concatenate([result, powered], axis=0), powered)
        result, powered = result + both[:extent], both[extent:]
    return result


def solve(inverse, incoming):
    high, low = halves(inverse)
    return (dot(high, incoming) + dot(low, incoming)).astype(BF16)


def onehot(a, b):
    return (a == b).astype(F32)


def body(
    process_rows, process_cols,
    matrix_hbm, one_hbm, two_hbm, piv_one, piv_two, out,
    matrix, head, tail, sent_sel, sel_in, item_in,
    sent_rows, pair_rows, group_rows, full_rows,
    l_sem, gh_send, gh_recv, fh_send, gt_send, gt_recv, ft_send, s_send, s_recv, i_send, i_recv,
    p_send, p_recv, q_send, q_recv, h_send, h_recv,
):
    width = piv_one.shape[1]
    rows_dev = matrix.shape[0]
    shard = one_hbm.shape[0]
    half = width // 2
    size_z = process_cols // 2
    groups = process_rows // 2
    my_row = lax.axis_index("prow")
    my_col = lax.axis_index("pcol")
    my_z, my_x = my_col // 2, my_col % 2
    x_peer = my_z * 2 + (1 - my_x)
    group, core = my_row // 2, my_row % 2
    pair = group * 2 + (1 - core)
    mesh_ids = pl.DeviceIdType.MESH

    def row_peer(step):
        return lax.rem(my_row + step, process_rows)

    def group_peer(step):
        return lax.rem(group + step, groups) * 2 + core

    def z_peer(step):
        return lax.rem(my_z + step, size_z) * 2 + my_x

    barrier = pltpu.get_barrier_semaphore()
    for step in range(1, process_rows):
        pl.semaphore_signal(barrier, 1, device_id={"prow": row_peer(step)}, device_id_type=mesh_ids)
    for step in range(1, size_z):
        pl.semaphore_signal(barrier, 1, device_id={"pcol": z_peer(step)}, device_id_type=mesh_ids)
    pl.semaphore_signal(barrier, 1, device_id={"pcol": x_peer}, device_id_type=mesh_ids)

    first, rest = pl.ds(0, width), pl.ds(width, rows_dev - width)
    loads = [
        pltpu.make_async_copy(one_hbm.at[:, first], head.at[0, my_col], l_sem.at[0]),
        pltpu.make_async_copy(one_hbm.at[:, rest], tail.at[0, my_col], l_sem.at[1]),
        pltpu.make_async_copy(two_hbm.at[:, first], head.at[1, my_col], l_sem.at[2]),
        pltpu.make_async_copy(matrix_hbm, matrix, l_sem.at[3]),
        pltpu.make_async_copy(two_hbm.at[:, rest], tail.at[1, my_col], l_sem.at[4]),
    ]
    for load in loads:
        load.start()

    local = lax.broadcasted_iota(jnp.int32, (rows_dev, width), 0)
    logical = (local // width * process_rows + my_row) * width + local % width
    hit_one = onehot(logical, piv_one[...])
    hit_two = onehot(logical, piv_two[...])
    pick_one, pick_two = hit_one.astype(BF16), hit_two.astype(BF16)
    for load in loads:
        load.wait()
    sent_sel[...] = (dot(head[0, my_col], pick_two[:width]) + dot(tail[0, my_col], pick_two[width:])).astype(BF16)

    pl.semaphore_wait(barrier, process_rows - 1 + size_z)

    def remote(src, dst, send, recv, device):
        return pltpu.make_async_remote_copy(
            src_ref=src, dst_ref=dst, send_sem=send, recv_sem=recv,
            device_id=device, device_id_type=mesh_ids,
        )

    def slot_of(piece, col):
        if piece < 3:
            return head.at[piece, col], gh_send.at[piece], gh_recv.at[piece, col], fh_send.at[piece]
        return tail.at[piece - 3, col], gt_send.at[piece - 3], gt_recv.at[piece - 3, col], ft_send.at[piece - 3]

    def gather_copy(piece, step):
        slot, send, recv, _ = slot_of(piece, my_col)
        return remote(slot, slot, send.at[step], recv, {"pcol": z_peer(step) if step else x_peer})

    def forward_copy(piece, step):
        slot, _, recv, send = slot_of(piece, z_peer(step))
        return remote(slot, slot, send.at[step], recv, {"pcol": x_peer})

    def gather(piece):
        for step in range(size_z):
            gather_copy(piece, step).start()

    def arrive(piece, col):
        slot, send, recv, _ = slot_of(piece, col)
        remote(slot, slot, send.at[0], recv, {"pcol": x_peer}).wait_recv()

    def take_z(piece):
        for step in range(1, size_z):
            arrive(piece, z_peer(step))
            forward_copy(piece, step).start()

    def take_x(piece):
        for step in range(size_z):
            arrive(piece, lax.rem(my_z + step, size_z) * 2 + (1 - my_x))

    def flat(block):
        return block.reshape(process_cols * shard, block.shape[-1])

    def sel_copy(step):
        return remote(sent_sel, sel_in.at[my_row], s_send.at[step], s_recv.at[my_row], {"prow": row_peer(step)})

    owners = (0, 1, 1, 0, 1)

    def item_source(item):
        if item < 3:
            return head.at[(0, 1, 0)[item]]
        return matrix.at[first, :]

    def item_place(item):
        return item_in[0].at[item] if item < 3 else item_in[1].at[item - 3]

    def item_copy(item, step, source):
        device = {"prow": group_peer(step) if step else pair}
        return remote(source, item_place(item), i_send.at[item, step], i_recv.at[item], device)

    def send_item(item):
        @pl.when(my_row == owners[item])
        def _():
            for step in range(groups):
                item_copy(item, step, item_source(item)).start()
            if item < 3:
                item_in[0][item] = head[(0, 1, 0)[item]]
            else:
                item_in[1][item - 3] = matrix[first, :]

    def take_item(item):
        @pl.when(my_row != owners[item])
        def _():
            item_copy(item, 0, item_place(item)).wait_recv()

        @pl.when((group > 0) & (core == owners[item]))
        def _():
            item_copy(item, 0, item_place(item)).start()

    def pair_copy(which):
        return remote(sent_rows.at[which, 1 - core], pair_rows.at[which], p_send.at[which], p_recv.at[which], {"prow": pair})

    def group_copy(which, step):
        return remote(
            sent_rows.at[which, core], group_rows.at[which, group],
            q_send.at[which, step], q_recv.at[which, group], {"prow": group_peer(step)},
        )

    def half_copy(which):
        return remote(
            full_rows.at[which, core], full_rows.at[which, core], h_send.at[which], h_recv.at[which], {"prow": pair}
        )

    def sum_pair(which):
        slot = pair_rows.at[which]
        remote(slot, slot, p_send.at[which], p_recv.at[which], {"prow": pair}).wait_recv()
        total = sent_rows[which, core].astype(F32) + pair_rows[which].astype(F32)
        sent_rows[which, core] = total.astype(BF16)
        for step in range(1, groups):
            group_copy(which, step).start()

    def sum_groups(which):
        total = sent_rows[which, core].astype(F32)
        for step in range(1, groups):
            source = lax.rem(group + step, groups)
            slot = group_rows.at[which, source]
            remote(slot, slot, q_send.at[which, 0], q_recv.at[which, source], {"prow": pair}).wait_recv()
            total = total + group_rows[which, source].astype(F32)
        full_rows[which, core] = total.astype(BF16)
        half_copy(which).start()

    def chosen(which):
        slot = full_rows.at[which, 1 - core]
        remote(slot, slot, h_send.at[which], h_recv.at[which], {"prow": pair}).wait_recv()
        return full_rows[which].reshape(width, full_rows.shape[-1])

    peers = range(1, process_rows)
    gather(0)
    gather(1)
    for step in peers:
        sel_copy(step).start()
    for which, pick in enumerate((pick_one, pick_two)):
        sent_rows[which] = dot_t(pick, matrix[...]).astype(BF16).reshape(2, half, matrix.shape[1])
        pair_copy(which).start()
    gather(3)
    take_z(0)
    take_z(1)
    sum_pair(0)
    sum_pair(1)
    selected = sent_sel[...].astype(F32)
    for step in peers:
        source = row_peer(step)
        slot = sel_in.at[source]
        remote(slot, slot, s_send.at[0], s_recv.at[source], {"prow": source}).wait_recv()
        selected = selected + sel_in[source].astype(F32)
    head[2, my_col] = selected.astype(BF16)
    gather(2)
    gather(4)
    take_x(0)
    send_item(0)
    take_x(1)
    send_item(1)
    sum_groups(0)
    sum_groups(1)
    send_item(3)
    send_item(2)
    send_item(4)
    take_z(3)
    take_z(2)
    take_item(0)
    take_item(1)
    inverse_one = unit_inverse(flat(item_in[0][0]))
    take_z(4)
    inverse_two = unit_inverse(flat(item_in[0][1]))
    take_item(3)
    take_item(2)
    take_item(4)

    solved_one = solve(inverse_one, chosen(0))
    leaving_one = item_in[1][0]

    first_across = jnp.broadcast_to(piv_one[...], (width, width))
    second_down = jnp.broadcast_to(piv_two[...].astype(F32), (width, width)).T.astype(jnp.int32)
    block_down = width + lax.broadcasted_iota(jnp.int32, (width, width), 0)

    def after_one(base, names, columns):
        match = onehot(names, first_across)
        moved = jnp.sum(match, axis=1, keepdims=True)
        swapped = base.astype(F32) * (1.0 - moved) + dot(match.astype(BF16), leaving_one)
        return (swapped - dot_t(columns, solved_one)).astype(BF16)

    take_x(2)
    incoming_two = after_one(chosen(1), second_down, flat(head[2]))
    leaving_two = after_one(item_in[1][1], block_down, flat(item_in[0][2]))
    solved_two = solve(inverse_two, incoming_two)

    moved_one = jnp.sum(hit_one, axis=1, keepdims=True)
    moved_two = jnp.sum(hit_two, axis=1, keepdims=True)
    swapped = matrix[...].astype(F32) * (1.0 - moved_one) + dot(pick_one, leaving_one)

    def times(which, solved):
        return jnp.concatenate([dot_t(flat(head[which]), solved), dot_t(flat(tail[which]), solved)], axis=0)

    take_x(3)
    current = (swapped - times(0, solved_one)).astype(BF16).astype(F32)
    swapped = current * (1.0 - moved_two) + dot(pick_two, leaving_two)
    take_x(4)
    out[...] = (swapped - times(1, solved_two)).astype(BF16)

    @pl.when(my_row == 0)
    def _():
        out[first, :] = solved_one

    @pl.when(my_row == 1)
    def _():
        out[first, :] = solved_two

    for step in peers:
        sel_copy(step).wait_send()
    for piece in range(5):
        for step in range(size_z):
            gather_copy(piece, step).wait_send()
        for step in range(1, size_z):
            forward_copy(piece, step).wait_send()
    for which in range(2):
        pair_copy(which).wait_send()
        half_copy(which).wait_send()
        for step in range(1, groups):
            group_copy(which, step).wait_send()
    for item in range(5):
        @pl.when(my_row == owners[item])
        def _(item=item):
            for step in range(groups):
                item_copy(item, step, item_source(item)).wait_send()

        @pl.when((group > 0) & (core == owners[item]))
        def _(item=item):
            item_copy(item, 0, item_place(item)).wait_send()


def on_device(matrix, panel_one, panel_two, pivots_one, pivots_two):
    process_rows = lax.axis_size("prow")
    process_cols = lax.axis_size("pcol")
    shard, rows_dev = panel_one.shape
    width = pivots_one.shape[0]
    cols = matrix.shape[1]
    vmem = pl.BlockSpec(memory_space=pltpu.VMEM)
    hbm = pl.BlockSpec(memory_space=pltpu.HBM)
    dma = pltpu.SemaphoreType.DMA
    assert rows_dev > width and shard * process_cols == width
    assert process_cols % 2 == 0 and process_rows % 2 == 0
    size_z = process_cols // 2
    groups = process_rows // 2
    half = width // 2
    return pl.pallas_call(
        functools.partial(body, process_rows, process_cols),
        out_shape=jax.ShapeDtypeStruct(matrix.shape, BF16),
        in_specs=[hbm] * 3 + [vmem] * 2,
        out_specs=vmem,
        scratch_shapes=[
            pltpu.VMEM((rows_dev, cols), BF16),
            pltpu.VMEM((3, process_cols, shard, width), BF16),
            pltpu.VMEM((2, process_cols, shard, rows_dev - width), BF16),
            pltpu.VMEM((shard, width), BF16),
            pltpu.VMEM((process_rows, shard, width), BF16),
            [pltpu.VMEM((3, process_cols, shard, width), BF16), pltpu.VMEM((2, width, cols), BF16)],
            pltpu.VMEM((2, 2, half, cols), BF16),
            pltpu.VMEM((2, half, cols), BF16),
            pltpu.VMEM((2, groups, half, cols), BF16),
            pltpu.VMEM((2, 2, half, cols), BF16),
            dma((5,)),
            dma((3, size_z)), dma((3, process_cols)), dma((3, size_z)),
            dma((2, size_z)), dma((2, process_cols)), dma((2, size_z)),
            dma((process_rows,)), dma((process_rows,)),
            dma((5, groups)), dma((5,)),
            dma((2,)), dma((2,)),
            dma((2, groups)), dma((2, groups)),
            dma((2,)), dma((2,)),
        ],
        compiler_params=pltpu.CompilerParams(
            collective_id=0, has_side_effects=True, vmem_limit_bytes=40 * 1024 * 1024
        ),
    )(matrix, panel_one, panel_two, pivots_one.reshape(1, width), pivots_two.reshape(1, width))


def solution(mesh):
    placed = (P("prow", "pcol"), P("pcol", "prow"), P("pcol", "prow"), P(), P())
    return jax.shard_map(
        on_device, mesh=mesh, in_specs=placed, out_specs=P("prow", "pcol"), check_vma=False
    )
```

time: 41.3 us -> 36.6 us (0.89); the launches traced: 40.5 us -> 36.3 us
  Pallas kernels: 36.3 us -> 32.1 us
    pallas_call x1, Pallas kernels: 36.3 us -> 32.1 us  [on_device(): pl.pallas_call(functools.partial(body, process_rows, process_cols), out_s...]
where the time goes in v2:
time: 36.6 us; the launch traced here: 36.3 us
  Pallas kernels  32.1 us (88%)
  local copies, waits for them, and re-layouts  4.21 us (12%)
    pallas_call x1, Pallas kernels, on_device(): pl.pallas_call(functools.partial(body, process_rows, process_cols), out_s...  32.1 us
    unnamed x11, local copies, waits for them, and re-layouts  4.21 us

profile of v2, /device:TPU:12, one launch (start us, length us, event | category | flops | bytes accessed | tf_op | source)
XLA Modules:
  0.0 36.3 jit_solution(4888455019748936820)
XLA Ops:
  0.0 0.0 copy-start.4
  0.0 0.0 copy-start.3
  0.0 0.7 %copy-done.4 = s32[256]{0:T(256)S(1)} copy-done((s32[256]{0:T(256)S(1)}, s32[256]{0:T(256)}, u32[]{:S(2)}) %copy-start.4) | copy-done | bytes 1048
  0.7 0.0 copy-done.3
  0.7 0.0 copy-start
  0.7 1.0 %copy-done = bf16[1024,256]{1,0:T(8,128)(2,1)S(1)} copy-done((bf16[1024,256]{1,0:T(8,128)(2,1)S(1)}, bf16[1024,256]{1,0:T(8,128)(2,1)}, u32[]{:S(2)}) %copy-start) | copy-done | bytes 524312
  1.7 0.0 copy-start.1
  1.7 0.8 %copy-done.1 = bf16[32,1024]{1,0:T(8,128)(2,1)S(1)} copy-done((bf16[32,1024]{1,0:T(8,128)(2,1)S(1)}, bf16[32,1024]{1,0:T(8,128)(2,1)}, u32[]{:S(2)}) %copy-start.1) | copy-done | bytes 65560
  2.6 0.0 copy-start.2
  2.6 0.8 %copy-done.2 = bf16[32,1024]{1,0:T(8,128)(2,1)S(1)} copy-done((bf16[32,1024]{1,0:T(8,128)(2,1)S(1)}, bf16[32,1024]{1,0:T(8,128)(2,1)}, u32[]{:S(2)}) %copy-start.2) | copy-done | bytes 65560
  3.4 32.1 %shard_map.55 = bf16[1024,256]{1,0:T(8,128)(2,1)S(1)} custom-call(bf16[1024,256]{1,0:T(8,128)(2,1)S(1)} %copy-done, bf16[32,1024]{1,0:T(8,128)(2,1)S(1)} %copy-done.1, bf16[32,1024]{1,0:T(8,128)(2,1)S(1)} %copy-done.2, s32[1,256]{1,0:T(1,128)S(1)} %bitcast.2, s32[1,256]{1,0:T(1,128)S(1)} %bitcast.3), custom_call_target="tpu_custom_call" | custom-call | tf_op jit(solution)/shard_map/pallas_call | solution.py:350
  35.5 0.8 %copy.7 = bf16[1024,256]{1,0:T(8,128)(2,1)} copy(bf16[1024,256]{1,0:T(8,128)(2,1)S(1)} %shard_map.55) | data formatting | bytes 1048576
Async XLA Ops:
  0.0 0.7 %copy-start.4 = (s32[256]{0:T(256)S(1)}, s32[256]{0:T(256)}, u32[]{:S(2)}) copy-start(s32[256]{0:T(256)} %param.9) | copy-start | bytes 3076
  0.0 0.7 %copy-start.3 = (s32[256]{0:T(256)S(1)}, s32[256]{0:T(256)}, u32[]{:S(2)}) copy-start(s32[256]{0:T(256)} %param.8) | copy-start | bytes 3076
  0.7 1.0 %copy-start = (bf16[1024,256]{1,0:T(8,128)(2,1)S(1)}, bf16[1024,256]{1,0:T(8,128)(2,1)}, u32[]{:S(2)}) copy-start(bf16[1024,256]{1,0:T(8,128)(2,1)} %matrix_hbm.1) | copy-start | bytes 1572868
  1.7 0.8 %copy-start.1 = (bf16[32,1024]{1,0:T(8,128)(2,1)S(1)}, bf16[32,1024]{1,0:T(8,128)(2,1)}, u32[]{:S(2)}) copy-start(bf16[32,1024]{1,0:T(8,128)(2,1)} %one_hbm.1) | copy-start | bytes 196612
  2.6 0.8 %copy-start.2 = (bf16[32,1024]{1,0:T(8,128)(2,1)S(1)}, bf16[32,1024]{1,0:T(8,128)(2,1)}, u32[]{:S(2)}) copy-start(bf16[32,1024]{1,0:T(8,128)(2,1)} %two_hbm.1) | copy-start | bytes 196612

commit v3 on v2

--- a/solution.py
+++ b/solution.py
@@ -29,6 +29,22 @@
     a_high, a_low = halves(a)
     b_high, b_low = halves(b)
     return dot(a_high, b_high) + (dot(a_high, b_low) + dot(a_low, b_high))
+
+
+def unit_inverses(diagonals):
+    extent = diagonals[0].shape[0]
+    row = lax.broadcasted_iota(jnp.int32, (extent, extent), 0)
+    col = lax.broadcasted_iota(jnp.int32, (extent, extent), 1)
+    stricts = [jnp.where(row > col, d.astype(F32).T, 0.0) for d in diagonals]
+    powers = [dot(s.astype(BF16), s.astype(BF16)) for s in stricts]
+    results = [jnp.where(row == col, 1.0, 0.0) - s for s in stricts]
+    repeats = (extent - 1).bit_length() - 1
+    for repeat in range(repeats):
+        if repeat == repeats - 1:
+            return [r + dot_split(r, p) for r, p in zip(results, powers)]
+        both = [dot_split(jnp.concatenate([r, p], axis=0), p) for r, p in zip(results, powers)]
+        results = [r + b[:extent] for r, b in zip(results, both)]
+        powers = [b[extent:] for b in both]
 
 
 def unit_inverse(diagonal):
@@ -264,9 +280,8 @@
     take_z(2)
     take_item(0)
     take_item(1)
-    inverse_one = unit_inverse(flat(item_in[0][0]))
     take_z(4)
-    inverse_two = unit_inverse(flat(item_in[0][1]))
+    inverse_one, inverse_two = unit_inverses([flat(item_in[0][0]), flat(item_in[0][1])])
     take_item(3)
     take_item(2)
     take_item(4)
@@ -373,7 +388,7 @@
             dma((2,)), dma((2,)),
         ],
         compiler_params=pltpu.CompilerParams(
-            collective_id=0, has_side_effects=True, vmem_limit_bytes=40 * 1024 * 1024
+            collective_id=0, has_side_effects=True, vmem_limit_bytes=63 * 1024 * 1024
         ),
     )(matrix, panel_one, panel_two, pivots_one.reshape(1, width), pivots_two.reshape(1, width))
 

time: 36.6 us -> 32 us (0.87)
  local copies, waits for them, and re-layouts: 4.21 us -> 1.87 us
  Pallas kernels: 32.1 us -> 30 us
    unnamed x11 -> x1, local copies, waits for them, and re-layouts: 4.21 us -> 1.87 us
    pallas_call x1, Pallas kernels: 32.1 us -> 30 us  [on_device(): pl.pallas_call(functools.partial(body, process_rows, process_cols), out_s...]
where the time goes in v3:
time: 32 us; the launch traced here: 31.8 us
  Pallas kernels  30 us (94%)
  local copies, waits for them, and re-layouts  1.87 us (6%)
    pallas_call x1, Pallas kernels, on_device(): pl.pallas_call(functools.partial(body, process_rows, process_cols), out_s...  30 us
    unnamed x1, local copies, waits for them, and re-layouts  1.87 us

profile of v3, /device:TPU:12, one launch (start us, length us, event | category | flops | bytes accessed | tf_op | source)
XLA Modules:
  0.0 31.8 jit_solution(6150707000788172043)
XLA Ops:
  0.0 30.0 %shard_map.55 = bf16[1024,256]{1,0:T(8,128)(2,1)} custom-call(bf16[1024,256]{1,0:T(8,128)(2,1)} %matrix_hbm.1, bf16[32,1024]{1,0:T(8,128)(2,1)} %one_hbm.1, bf16[32,1024]{1,0:T(8,128)(2,1)} %two_hbm.1, s32[1,256]{1,0:T(1,128)} %bitcast.2, s32[1,256]{1,0:T(1,128)} %bitcast.3), custom_call_target="tpu_custom_call" | custom-call | tf_op jit(solution)/shard_map/pallas_call | solution.py:365
  30.0 1.9 %copy.7 = bf16[1024,256]{1,0:T(8,128)(2,1)} copy(bf16[1024,256]{1,0:T(8,128)(2,1)} %shard_map.55) | data formatting | bytes 1048576

commit v4 on v3

--- a/solution.py
+++ b/solution.py
@@ -75,8 +75,8 @@
 
 def body(
     process_rows, process_cols,
-    matrix_hbm, one_hbm, two_hbm, piv_one, piv_two, out,
-    matrix, head, tail, sent_sel, sel_in, item_in,
+    matrix_hbm, one_hbm, two_hbm, piv_one_hbm, piv_two_hbm, out,
+    piv_one, piv_two, matrix, head, tail, sent_sel, sel_in, item_in,
     sent_rows, pair_rows, group_rows, full_rows,
     l_sem, gh_send, gh_recv, fh_send, gt_send, gt_recv, ft_send, s_send, s_recv, i_send, i_recv,
     p_send, p_recv, q_send, q_recv, h_send, h_recv,
@@ -119,8 +119,17 @@
         pltpu.make_async_copy(matrix_hbm, matrix, l_sem.at[3]),
         pltpu.make_async_copy(two_hbm.at[:, rest], tail.at[1, my_col], l_sem.at[4]),
     ]
+    names = [
+        pltpu.make_async_copy(piv_one_hbm, piv_one, l_sem.at[5]),
+        pltpu.make_async_copy(piv_two_hbm, piv_two, l_sem.at[6]),
+    ]
+    for load in names:
+        load.start()
     for load in loads:
         load.start()
+
+    for load in names:
+        load.wait()
 
     local = lax.broadcasted_iota(jnp.int32, (rows_dev, width), 0)
     logical = (local // width * process_rows + my_row) * width + local % width
@@ -130,6 +139,8 @@
     for load in loads:
         load.wait()
     sent_sel[...] = (dot(head[0, my_col], pick_two[:width]) + dot(tail[0, my_col], pick_two[width:])).astype(BF16)
+    for which, pick in enumerate((pick_one, pick_two)):
+        sent_rows[which] = dot_t(pick, matrix[...]).astype(BF16).reshape(2, half, matrix.shape[1])
 
     pl.semaphore_wait(barrier, process_rows - 1 + size_z)
 
@@ -153,7 +164,7 @@
         return remote(slot, slot, send.at[step], recv, {"pcol": x_peer})
 
     def gather(piece):
-        for step in range(size_z):
+        for step in reversed(range(size_z)):
             gather_copy(piece, step).start()
 
     def arrive(piece, col):
@@ -250,8 +261,7 @@
     gather(1)
     for step in peers:
         sel_copy(step).start()
-    for which, pick in enumerate((pick_one, pick_two)):
-        sent_rows[which] = dot_t(pick, matrix[...]).astype(BF16).reshape(2, half, matrix.shape[1])
+    for which in range(2):
         pair_copy(which).start()
     gather(3)
     take_z(0)
@@ -365,9 +375,11 @@
     return pl.pallas_call(
         functools.partial(body, process_rows, process_cols),
         out_shape=jax.ShapeDtypeStruct(matrix.shape, BF16),
-        in_specs=[hbm] * 3 + [vmem] * 2,
+        in_specs=[hbm] * 5,
         out_specs=vmem,
         scratch_shapes=[
+            pltpu.VMEM((1, width), jnp.int32),
+            pltpu.VMEM((1, width), jnp.int32),
             pltpu.VMEM((rows_dev, cols), BF16),
             pltpu.VMEM((3, process_cols, shard, width), BF16),
             pltpu.VMEM((2, process_cols, shard, rows_dev - width), BF16),
@@ -378,7 +390,7 @@
             pltpu.VMEM((2, half, cols), BF16),
             pltpu.VMEM((2, groups, half, cols), BF16),
             pltpu.VMEM((2, 2, half, cols), BF16),
-            dma((5,)),
+            dma((7,)),
             dma((3, size_z)), dma((3, process_cols)), dma((3, size_z)),
             dma((2, size_z)), dma((2, process_cols)), dma((2, size_z)),
             dma((process_rows,)), dma((process_rows,)),

time: 32 us -> 31 us (0.969)
  the two profiles are of different devices: /device:TPU:12 before, /device:TPU:4 now
where the time goes in v4:
time: 31 us; the launch traced here: 30.8 us
  Pallas kernels  29 us (94%)
  local copies, waits for them, and re-layouts  1.87 us (6%)
    pallas_call x1, Pallas kernels, on_device(): pl.pallas_call(functools.partial(body, process_rows, process_cols), out_s...  29 us
    unnamed x1, local copies, waits for them, and re-layouts  1.87 us

profile of v4, /device:TPU:4, one launch (start us, length us, event | category | flops | bytes accessed | tf_op | source)
XLA Modules:
  0.0 30.8 jit_solution(7282431881145931086)
XLA Ops:
  0.0 29.0 %shard_map.55 = bf16[1024,256]{1,0:T(8,128)(2,1)} custom-call(bf16[1024,256]{1,0:T(8,128)(2,1)} %matrix_hbm.1, bf16[32,1024]{1,0:T(8,128)(2,1)} %one_hbm.1, bf16[32,1024]{1,0:T(8,128)(2,1)} %two_hbm.1, s32[1,256]{1,0:T(1,128)} %bitcast.2, s32[1,256]{1,0:T(1,128)} %bitcast.3), custom_call_target="tpu_custom_call" | custom-call | tf_op jit(solution)/shard_map/pallas_call | solution.py:375
  29.0 1.9 %copy.7 = bf16[1024,256]{1,0:T(8,128)(2,1)} copy(bf16[1024,256]{1,0:T(8,128)(2,1)} %shard_map.55) | data formatting | bytes 1048576
